TPU v7x, 32 devices: a whole 2x2x4 slice. The times are simulated.
32 devices in a mesh: twin: 2 (over x), dp: 16 (over z, y, core).
Axes of the slice: x: 2, y: 2, z: 4, core: 2. Of those that a mesh axis runs over, the one named last changes fastest.
Arguments:
- hidden: bfloat16 [64, 512, 768], P(('twin', 'dp')), may hold values from -6 to 6
- segment_ids: int32 [64, 512], P(('twin', 'dp')), may hold values from 0 to 7, never falling along the last dimension, each value on 1 to 128 neighbouring positions
- targets: int32 [256], replicated, may hold values from 0 to 255, each once
- w_qkv: bfloat16 [768, 2304], replicated, may hold values from -0.21875 to 0.21875
- b_query: bfloat16 [768], replicated, may hold values from -3 to 3
- b_value: bfloat16 [768], replicated, may hold values from -3 to 3
- w_out: bfloat16 [768, 768], replicated, may hold values from -1.25 to 1.25
- b_out: bfloat16 [768], replicated, may hold values from -3 to 3
- ln1_gain: bfloat16 [768], replicated, may hold values from 0.5 to 1.5
- ln1_bias: bfloat16 [768], replicated, may hold values from -2 to 2
- w_in: bfloat16 [768, 3072], replicated, may hold values from -0.21875 to 0.21875
- b_in: bfloat16 [3072], replicated, may hold values from -3 to 3
- w_down: bfloat16 [3072, 768], replicated, may hold values from -0.109375 to 0.109375
- b_down: bfloat16 [768], replicated, may hold values from -3 to 3
- ln2_gain: bfloat16 [768], replicated, may hold values from 0.5 to 1.5
- ln2_bias: bfloat16 [768], replicated, may hold values from -0.29882812 to 0.29882812
Outputs:
- losses: float32 [256], P(('twin', 'dp'))
- hidden_grad: bfloat16 [64, 512, 768], P(('twin', 'dp'))
- grad_w_qkv: float32 [768, 2304], P('dp')
- grad_b_query: float32 [768], P('dp')
- grad_b_value: float32 [768], P('dp')
- grad_w_out: float32 [768, 768], P('dp')
- grad_b_out: float32 [768], P('dp')
- grad_ln1_gain: float32 [768], P('dp')
- grad_ln1_bias: float32 [768], P('dp')
- grad_w_in: float32 [768, 3072], P('dp')
- grad_b_in: float32 [3072], P('dp')
- grad_w_down: float32 [3072, 768], P('dp')
- grad_b_down: float32 [768], P('dp')
- grad_ln2_gain: float32 [768], P('dp')
- grad_ln2_bias: float32 [768], P('dp')
Inputs may be any that keep to these rules, and one draw needn't show every extreme that they name: `segment_ids`: in each row the ids never fall; every id of 0 to 7 occurs, on 1 to 128 tokens. `targets`: every positive is the target of exactly one anchor.
All inputs are finite; a program needn't handle non-finite values.
Results may differ from a plain program's by a relative error of at most 0.012.
Values may be sent and summed in bfloat16 or wider, within the bound.
No kernel may reach another device: no remote copies, remote signals or barrier semaphores. Data moves between devices by JAX's collectives and lax.ppermute only.
A program may use at most 192 MiB of HBM per device.

v0:
```python
import jax
import jax.numpy as jnp
from jax import lax
from jax.sharding import PartitionSpec as P

D = 768
HEADS = 12
HEAD_DIM = 64
SEG = 8
cosine_scale = 64.0
loss_scale = 32.0
norm_epsilon = 1e-12
unit_epsilon = 1e-06
masked_score = -1e30


def layer_norm(inputs, norm_gain, norm_shift):
    middle = jnp.mean(inputs, axis=-1, keepdims=True)
    centered = inputs - middle
    spread = jnp.mean(centered * centered, axis=-1, keepdims=True)
    return centered * lax.rsqrt(spread + norm_epsilon) * norm_gain + norm_shift


def gelu_exact(inputs):
    return 0.5 * inputs * (1.0 + lax.erf(inputs * 0.5**0.5))


def contract_rows(left, right):
    return lax.dot_general(
        left, right, (((0,), (0,)), ((), ())), preferred_element_type=jnp.float32
    )


def contract_cols(left, right):
    return lax.dot_general(
        left, right, (((1,), (1,)), ((), ())), preferred_element_type=jnp.float32
    )


def split_heads(row_qkv):
    length = row_qkv.shape[0]
    query_heads = row_qkv[:, :D].reshape(length, HEADS, HEAD_DIM)
    key_heads = row_qkv[:, D : 2 * D].reshape(length, HEADS, HEAD_DIM)
    value_heads = row_qkv[:, 2 * D :].reshape(length, HEADS, HEAD_DIM)
    return (query_heads, key_heads, value_heads)


def masked_scores(query_heads, key_heads, row_seg):
    scores = jnp.einsum(
        "qhd,khd->hqk", query_heads, key_heads, preferred_element_type=jnp.float32
    ) * HEAD_DIM ** (-0.5)
    same_doc = (row_seg[:, None] == row_seg[None, :])[None]
    return (jnp.where(same_doc, scores, masked_score), same_doc)


def rank_loss(sims, wanted):
    row_top = jnp.max(sims, axis=1, keepdims=True)
    weights = jnp.exp(sims - row_top)
    row_total = jnp.sum(weights, axis=1, keepdims=True)
    column = lax.broadcasted_iota(jnp.int32, sims.shape, 1)
    target_hit = column == wanted[:, None]
    picked = jnp.sum(jnp.where(target_hit, sims, 0.0), axis=1)
    losses = row_top[:, 0] + jnp.log(row_total[:, 0]) - picked
    slope = (loss_scale * (weights / row_total - target_hit.astype(jnp.float32))).astype(
        jnp.bfloat16
    )
    return (losses, slope)


def body(
    hidden,
    segment_ids,
    targets,
    w_qkv,
    b_query,
    b_value,
    w_out,
    b_out,
    ln1_gain,
    ln1_bias,
    w_in,
    b_in,
    w_down,
    b_down,
    ln2_gain,
    ln2_bias,
):
    row_count, length, width = hidden.shape
    token_count = row_count * length
    tokens = hidden.reshape(token_count, width)
    bias_qkv = jnp.concatenate(
        [b_query.astype(jnp.float32), jnp.zeros((width,), jnp.float32), b_value.astype(jnp.float32)]
    )
    qkv_all = (jnp.dot(tokens, w_qkv, preferred_element_type=jnp.float32) + bias_qkv).astype(
        jnp.bfloat16
    )
    qkv_rows = qkv_all.reshape(row_count, length, 3 * width)

    def attend_forward(row_pack):
        row_qkv, row_seg = row_pack
        query_heads, key_heads, value_heads = split_heads(row_qkv)
        scores, same_doc = masked_scores(query_heads, key_heads, row_seg)
        row_top = jnp.max(scores, axis=-1, keepdims=True)
        weights = jnp.exp(scores - row_top)
        row_total = jnp.sum(weights, axis=-1, keepdims=True)
        prob_rows = (weights / row_total).astype(jnp.bfloat16)
        context = jnp.einsum(
            "hqk,khd->qhd", prob_rows, value_heads, preferred_element_type=jnp.float32
        )
        return (context.reshape(length, width).astype(jnp.bfloat16), row_top + jnp.log(row_total))

    context, log_total = lax.map(attend_forward, (qkv_rows, segment_ids))
    context_flat = context.reshape(token_count, width)
    attended = jnp.dot(context_flat, w_out, preferred_element_type=jnp.float32) + b_out.astype(
        jnp.float32
    )
    normed_one, norm_one_back = jax.vjp(
        layer_norm,
        tokens.astype(jnp.float32) + attended,
        ln1_gain.astype(jnp.float32),
        ln1_bias.astype(jnp.float32),
    )
    normed_low = normed_one.astype(jnp.bfloat16)
    hidden_pre = jnp.dot(normed_low, w_in, preferred_element_type=jnp.float32) + b_in.astype(
        jnp.float32
    )
    active, gelu_back = jax.vjp(gelu_exact, hidden_pre)
    active_low = active.astype(jnp.bfloat16)
    branch = jnp.dot(active_low, w_down, preferred_element_type=jnp.float32) + b_down.astype(
        jnp.float32
    )
    output, norm_two_back = jax.vjp(
        layer_norm, normed_one + branch, ln2_gain.astype(jnp.float32), ln2_bias.astype(jnp.float32)
    )
    member = (segment_ids[:, None, :] == jnp.arange(SEG, dtype=jnp.int32)[None, :, None]).astype(
        jnp.float32
    )
    counts = jnp.sum(member, axis=2, keepdims=True)

    def pool_units(out_rows):
        pooled = (
            jnp.einsum("rsl,rld->rsd", member, out_rows, precision=lax.Precision.HIGHEST) / counts
        )
        unit_rows = pooled * lax.rsqrt(
            jnp.mean(pooled * pooled, axis=-1, keepdims=True) + unit_epsilon
        )
        return unit_rows.reshape(row_count * SEG, width)

    unit_rows, pool_back = jax.vjp(pool_units, output.reshape(row_count, length, width))
    unit_low = unit_rows.astype(jnp.bfloat16)
    gathered = lax.all_gather(unit_low, ("twin", "dp"), axis=0, tiled=True)
    anchor_count = gathered.shape[0] // 2
    anchors = gathered[:anchor_count]
    positives = gathered[anchor_count:]
    factor = cosine_scale / width
    devices = lax.axis_size(("twin", "dp"))
    loss_share = anchor_count // devices
    loss_start = lax.axis_index(("twin", "dp")) * loss_share
    all_losses, slope = rank_loss(contract_cols(anchors, positives) * factor, targets)
    losses = lax.dynamic_slice_in_dim(all_losses, loss_start, loss_share, 0)
    sentences = unit_low.shape[0]
    offset = lax.axis_index("dp") * sentences
    anchor_rows = (
        jnp.dot(
            lax.dynamic_slice_in_dim(slope, offset, sentences, 0),
            positives,
            preferred_element_type=jnp.float32,
        )
        * factor
    )
    positive_rows = (
        contract_rows(lax.dynamic_slice_in_dim(slope, offset, sentences, 1), anchors) * factor
    )
    unit_grad = jnp.where(lax.axis_index("twin") == 0, anchor_rows, positive_rows)
    grad_output = pool_back(unit_grad)[0].reshape(token_count, width)
    grad_sum_two, grad_ln2_gain, grad_ln2_bias = norm_two_back(grad_output)
    grad_branch = grad_sum_two.astype(jnp.bfloat16)
    grad_w_down = contract_rows(active_low, grad_branch)
    grad_b_down = jnp.sum(grad_branch, axis=0, dtype=jnp.float32)
    grad_active = contract_cols(grad_branch, w_down)
    grad_pre = gelu_back(grad_active)[0].astype(jnp.bfloat16)
    grad_w_in = contract_rows(normed_low, grad_pre)
    grad_b_in = jnp.sum(grad_pre, axis=0, dtype=jnp.float32)
    grad_normed = contract_cols(grad_pre, w_in) + grad_sum_two
    grad_sum_one, grad_ln1_gain, grad_ln1_bias = norm_one_back(grad_normed)
    grad_attended = grad_sum_one.astype(jnp.bfloat16)
    grad_w_out = contract_rows(context_flat, grad_attended)
    grad_b_out = jnp.sum(grad_attended, axis=0, dtype=jnp.float32)
    grad_context = (
        contract_cols(grad_attended, w_out).astype(jnp.bfloat16).reshape(row_count, length, width)
    )

    def attend_backward(row_pack):
        row_qkv, row_seg, row_lse, row_grad = row_pack
        query_heads, key_heads, value_heads = split_heads(row_qkv)
        scores, same_doc = masked_scores(query_heads, key_heads, row_seg)
        prob_rows = jnp.where(same_doc, jnp.exp(scores - row_lse), 0.0)
        grad_heads = row_grad.reshape(length, HEADS, HEAD_DIM)
        grad_value = jnp.einsum(
            "hqk,qhd->khd",
            prob_rows.astype(jnp.bfloat16),
            grad_heads,
            preferred_element_type=jnp.float32,
        )
        grad_prob = jnp.einsum(
            "qhd,khd->hqk", grad_heads, value_heads, preferred_element_type=jnp.float32
        )
        inner = jnp.sum(prob_rows * grad_prob, axis=-1, keepdims=True)
        grad_scores = (prob_rows * (grad_prob - inner)).astype(jnp.bfloat16)
        grad_query = jnp.einsum(
            "hqk,khd->qhd", grad_scores, key_heads, preferred_element_type=jnp.float32
        ) * HEAD_DIM ** (-0.5)
        grad_key = jnp.einsum(
            "hqk,qhd->khd", grad_scores, query_heads, preferred_element_type=jnp.float32
        ) * HEAD_DIM ** (-0.5)
        return jnp.concatenate(
            [
                grad_query.reshape(length, width),
                grad_key.reshape(length, width),
                grad_value.reshape(length, width),
            ],
            axis=1,
        ).astype(jnp.bfloat16)

    grad_qkv = lax.map(attend_backward, (qkv_rows, segment_ids, log_total, grad_context))
    grad_qkv = grad_qkv.reshape(token_count, 3 * width)
    grad_w_qkv = contract_rows(tokens, grad_qkv)
    grad_b_query = jnp.sum(grad_qkv[:, :width], axis=0, dtype=jnp.float32)
    grad_b_value = jnp.sum(grad_qkv[:, 2 * width :], axis=0, dtype=jnp.float32)
    hidden_grad = (
        (contract_cols(grad_qkv, w_qkv) + grad_sum_one)
        .astype(jnp.bfloat16)
        .reshape(row_count, length, width)
    )
    (
        grad_w_qkv,
        grad_b_query,
        grad_b_value,
        grad_w_out,
        grad_b_out,
        grad_ln1_gain,
        grad_ln1_bias,
        grad_w_in,
        grad_b_in,
        grad_w_down,
        grad_b_down,
        grad_ln2_gain,
        grad_ln2_bias,
    ) = (
        lax.psum_scatter(grad_w_qkv, "dp", scatter_dimension=0, tiled=True),
        lax.psum_scatter(grad_b_query, "dp", scatter_dimension=0, tiled=True),
        lax.psum_scatter(grad_b_value, "dp", scatter_dimension=0, tiled=True),
        lax.psum_scatter(grad_w_out, "dp", scatter_dimension=0, tiled=True),
        lax.psum_scatter(grad_b_out, "dp", scatter_dimension=0, tiled=True),
        lax.psum_scatter(grad_ln1_gain, "dp", scatter_dimension=0, tiled=True),
        lax.psum_scatter(grad_ln1_bias, "dp", scatter_dimension=0, tiled=True),
        lax.psum_scatter(grad_w_in, "dp", scatter_dimension=0, tiled=True),
        lax.psum_scatter(grad_b_in, "dp", scatter_dimension=0, tiled=True),
        lax.psum_scatter(grad_w_down, "dp", scatter_dimension=0, tiled=True),
        lax.psum_scatter(grad_b_down, "dp", scatter_dimension=0, tiled=True),
        lax.psum_scatter(grad_ln2_gain, "dp", scatter_dimension=0, tiled=True),
        lax.psum_scatter(grad_ln2_bias, "dp", scatter_dimension=0, tiled=True),
    )
    (
        grad_w_qkv,
        grad_b_query,
        grad_b_value,
        grad_w_out,
        grad_b_out,
        grad_ln1_gain,
        grad_ln1_bias,
        grad_w_in,
        grad_b_in,
        grad_w_down,
        grad_b_down,
        grad_ln2_gain,
        grad_ln2_bias,
    ) = (
        lax.psum(grad_w_qkv.astype(jnp.bfloat16), "twin").astype(jnp.float32),
        lax.psum(grad_b_query.astype(jnp.bfloat16), "twin").astype(jnp.float32),
        lax.psum(grad_b_value.astype(jnp.bfloat16), "twin").astype(jnp.float32),
        lax.psum(grad_w_out.astype(jnp.bfloat16), "twin").astype(jnp.float32),
        lax.psum(grad_b_out.astype(jnp.bfloat16), "twin").astype(jnp.float32),
        lax.psum(grad_ln1_gain.astype(jnp.bfloat16), "twin").astype(jnp.float32),
        lax.psum(grad_ln1_bias.astype(jnp.bfloat16), "twin").astype(jnp.float32),
        lax.psum(grad_w_in.astype(jnp.bfloat16), "twin").astype(jnp.float32),
        lax.psum(grad_b_in.astype(jnp.bfloat16), "twin").astype(jnp.float32),
        lax.psum(grad_w_down.astype(jnp.bfloat16), "twin").astype(jnp.float32),
        lax.psum(grad_b_down.astype(jnp.bfloat16), "twin").astype(jnp.float32),
        lax.psum(grad_ln2_gain.astype(jnp.bfloat16), "twin").astype(jnp.float32),
        lax.psum(grad_ln2_bias.astype(jnp.bfloat16), "twin").astype(jnp.float32),
    )
    return (
        losses,
        hidden_grad,
        grad_w_qkv,
        grad_b_query,
        grad_b_value,
        grad_w_out,
        grad_b_out,
        grad_ln1_gain,
        grad_ln1_bias,
        grad_w_in,
        grad_b_in,
        grad_w_down,
        grad_b_down,
        grad_ln2_gain,
        grad_ln2_bias,
    )


def solution(mesh):
    placed = (
        P(("twin", "dp"), None, None),
        P(("twin", "dp"), None),
        P(),
        P(),
        P(),
        P(),
        P(),
        P(),
        P(),
        P(),
        P(),
        P(),
        P(),
        P(),
        P(),
        P(),
    )
    return jax.shard_map(
        body,
        mesh=mesh,
        in_specs=placed,
        out_specs=(
            P(("twin", "dp")),
            P(("twin", "dp"), None, None),
            P("dp", None),
            P("dp"),
            P("dp"),
            P("dp", None),
            P("dp"),
            P("dp"),
            P("dp"),
            P("dp", None),
            P("dp"),
            P("dp", None),
            P("dp"),
            P("dp"),
            P("dp"),
        ),
        check_vma=False,
    )
```

profile of v0, /device:TPU:0, one launch (start us, length us, event | category | flops | bytes accessed | tf_op | source)
XLA Modules:
  0.0 667.8 jit_solution(16013698214673223419)
XLA Ops:
  9.2 7.3 %add_convert_fusion.1 = bf16[1024,2304]{1,0:T(8,128)(2,1)} fusion(bf16[1024,768]{1,0:T(8,128)(2,1)} %bitcast.178, bf16[768,2304]{1,0:T(8,128)(2,1)S(1)} %copy-done, f32[2304]{0:T(1024)S(1)} %pad_maximum_fusion), kind=kOutput, calls=%fused_computation.35 | convolution fusion | flops 3628597248 | bytes 9839616 | tf_op jit(solution)/shard_map/dot_general | solution.py:94
  16.5 6.7 copy.53
  23.8 38.7 %while.22 = (s32[]{:T(128)}, bf16[2,512,768]{2,1,0:T(8,128)(2,1)}, f32[2,12,512,1]{2,1,3,0:T(8,128)}, bf16[2,512,2304]{1,2,0:T(8,128)(2,1)}, s32[2,512]{1,0:T(2,128)S(1)}, /*index=5*/s32[]{:T(128)}) while((s32[]{:T(128)}, bf16[2,512,768]{2,1,0:T(8,128)(2,1)}, f32[2,12,512,1]{2,1,3,0:T(8,128)}, bf16[2,512,2304]{1,2,0:T(8,128)(2,1)}, ...), condition=%wide.region_3.4_spmd, body=%wide.region_0.3_spmd.sunk | while | flops 843704320 | bytes 55786600 | solution.py:112
  27.0 2.1 fusion.115
  29.1 3.5 fusion.116
  33.3 5.5 fusion.117
  38.8 2.3 copy.70
  41.1 2.1 constant_dynamic-update-slice_fusion.2
  46.3 2.1 fusion.115
  48.5 3.5 fusion.116
  52.6 5.5 fusion.117
  58.2 2.3 copy.70
  60.5 2.1 constant_dynamic-update-slice_fusion.2
  62.6 3.9 fusion.49
  67.9 9.4 %multiply_convert_fusion.3 = (bf16[1024,3072]{1,0:T(8,128)(2,1)S(1)}, f32[1024,3072]{1,0:T(8,128)}) fusion(f32[3072]{0:T(1024)S(1)} %convert_element_type.203, bf16[768,3072]{1,0:T(8,128)(2,1)S(1)} %bitcast.177, f32[1024,768]{1,0:T(8,128)S(1)} %get-tuple-element.228, f32[768]{0:T(1024)S(1)} %convert_element_type.201, f32[768]{0:T(1024)S(1)} %convert_element_type.200, ...), kind=kOutput, calls=%fused_computation.33 | convolution fusion | flops 4854644736 | bytes 26765312 | tf_op jit(solution)/shard_map/dot_general | solution.py:124
  77.3 5.5 fusion.50
  86.6 45.3 %all_gather.3 = bf16[512,768]{1,0:T(8,128)(2,1)S(1)} all-gather(bf16[16,768]{1,0:T(8,128)(2,1)S(1)} %fusion.29), channel_id=1, replica_groups=mesh['twin'=2,'dp'=16] {'twin','dp'}, dimensions={0}, use_global_device_ids=true | all-gather | bytes 811008 | tf_op jit(solution)/shard_map/all_gather | solution.py:151
  138.5 2.9 fusion.52
  145.8 15.0 %convert_reduce_fusion = (f32[3072]{0:T(1024)}, bf16[1024,3072]{1,0:T(8,128)(2,1)S(1)}) fusion(bf16[1024,768]{1,0:T(8,128)(2,1)S(1)} %get-tuple-element.210, bf16[3072,768]{1,0:T(8,128)(2,1)S(1)} %bitcast.175, f32[1024,3072]{1,0:T(8,128)} %get-tuple-element.230, f32[3072]{0:T(1024)S(1)} %copy-done.46), kind=kOutput, calls=%fused_computation.31 | convolution fusion | flops 4882166784 | bytes 25190400 | tf_op jit(solution)/shard_map/dot_general | solution.py:35
  160.8 11.3 %multiply_reduce_fusion.1 = (f32[768]{0:T(1024)}, f32[1024]{0:T(1024)S(1)}, f32[768]{0:T(1024)}, f32[1024,768]{1,0:T(8,128)S(1)}) fusion(f32[1024,768]{1,0:T(8,128)S(1)} %copy-done.9, f32[1024]{0:T(1024)S(1)} %fusion.36, f32[1024]{0:T(1024)S(1)} %broadcast_multiply_fusion.1, f32[768]{0:T(1024)S(1)} %convert_element_type.200, ...), kind=kOutput, calls=%fused_computation.43 | convolution fusion | flops 4839699456 | bytes 20472832 | tf_op jit(solution)/shard_map/dot_general | solution.py:35
  177.3 2.9 fusion.54
  180.2 4.3 convolution_convert_fusion
  184.5 85.6 %while.23 = (s32[]{:T(128)}, bf16[2,512,2304]{1,2,0:T(8,128)(2,1)}, bf16[2,512,2304]{1,2,0:T(8,128)(2,1)}, s32[2,512]{1,0:T(2,128)S(1)}, f32[2,12,512,1]{2,1,3,0...) while((s32[]{:T(128)}, bf16[2,512,2304]{1,2,0:T(8,128)(2,1)}, bf16[2,512,2304]{1,2,0:T(8,128)(2,1)}, ...), condition=%wide.region_20.21_spmd, body=%wide.region_18.20_spmd.sunk | while | flops 2079188992 | bytes 181877680 | solution.py:225
  187.9 6.4 fusion.129
  196.9 2.3 copy.71
  199.2 11.5 %multiply_reduce_fusion.9 = (f32[12,512]{1,0:T(8,128)S(1)}, f32[12,512,512]{1,2,0:T(8,128)}) fusion(f32[12,512]{1,0:T(8,128)} %dynamic-slice_bitcast_fusion.7, f32[12,512,512]{1,2,0:T(8,128)} %fusion.129, pred[512,512]{0,1:T(8,128)(4,1)} %broadcast_compare_fusion.5, bf16[512,12,64]{0,2,1:T(8,128)(2,1)} %bitcast.162, bf16[512,12,64]{0,2,1:T(8,128)(2,1)} %bitcast.160), kind=kOutput, calls=%fused_computation.15.clone.1 | convolution fusion | flops 421521408 | bytes 27049984 | tf_op jit(solution)/shard_map/while/body/eval_jaxpr/qhd,khd->hqk/dot_general | solution.py:205
  212.6 7.1 %multiply_convert_fusion.9 = bf16[12,512,512]{1,2,0:T(8,128)(2,1)S(1)} fusion(f32[12,512,512]{1,2,0:T(8,128)} %get-tuple-element.330, f32[12,512]{1,0:T(8,128)S(1)} %get-tuple-element.331, f32[12,512]{1,0:T(8,128)S(1)} %copy-done.15, f32[12,512,512]{1,2,0:T(8,128)S(1)} %bitcast.150, pred[512,512]{0,1:T(8,128)(4,1)S(1)} %copy-done.10), kind=kLoop, calls=%fused_computation.14.clone.1 | loop fusion | flops 22020096 | bytes 31768576 | tf_op jit(solution)/shard_map/while/body/eval_jaxpr/convert_element_type | solution.py:209
  220.9 2.0 multiply_convert_fusion.10
  223.0 3.2 fusion.130
  230.6 6.4 fusion.129
  239.5 2.3 copy.71
  241.8 11.5 %multiply_reduce_fusion.9 = (f32[12,512]{1,0:T(8,128)S(1)}, f32[12,512,512]{1,2,0:T(8,128)}) fusion(f32[12,512]{1,0:T(8,128)} %dynamic-slice_bitcast_fusion.7, f32[12,512,512]{1,2,0:T(8,128)} %fusion.129, pred[512,512]{0,1:T(8,128)(4,1)} %broadcast_compare_fusion.5, bf16[512,12,64]{0,2,1:T(8,128)(2,1)} %bitcast.162, bf16[512,12,64]{0,2,1:T(8,128)(2,1)} %bitcast.160), kind=kOutput, calls=%fused_computation.15.clone.1 | convolution fusion | flops 421521408 | bytes 27049984 | tf_op jit(solution)/shard_map/while/body/eval_jaxpr/qhd,khd->hqk/dot_general | solution.py:205
  254.9 7.1 %multiply_convert_fusion.9 = bf16[12,512,512]{1,2,0:T(8,128)(2,1)S(1)} fusion(f32[12,512,512]{1,2,0:T(8,128)} %get-tuple-element.330, f32[12,512]{1,0:T(8,128)S(1)} %get-tuple-element.331, f32[12,512]{1,0:T(8,128)S(1)} %copy-done.15, f32[12,512,512]{1,2,0:T(8,128)S(1)} %bitcast.150, pred[512,512]{0,1:T(8,128)(4,1)S(1)} %copy-done.10), kind=kLoop, calls=%fused_computation.14.clone.1 | loop fusion | flops 22020096 | bytes 31768576 | tf_op jit(solution)/shard_map/while/body/eval_jaxpr/convert_element_type | solution.py:209
  265.2 3.2 fusion.130
  270.1 9.5 %convolution_bitcast_fusion = f32[768,2304]{0,1:T(8,128)} fusion(bf16[2,512,2304]{1,2,0:T(8,128)(2,1)} %get-tuple-element.77, bf16[2,512,768]{2,1,0:T(8,128)(2,1)} %param.20), kind=kOutput, calls=%fused_computation.36 | convolution fusion | flops 3623878656 | bytes 13369344 | tf_op jit(solution)/shard_map/dot_general | solution.py:29
  279.7 8.0 %copy.63 = f32[768,2304]{1,0:T(8,128)} copy(f32[768,2304]{0,1:T(8,128)} %convolution_bitcast_fusion) | data formatting | bytes 14155776
  288.4 11.4 %fusion.41 = f32[768,3072]{1,0:T(8,128)} fusion(bf16[1024,3072]{1,0:T(8,128)(2,1)} %copy-done.14, f32[1024,768]{1,0:T(8,128)} %copy-done.8, f32[768]{0:T(1024)S(1)} %copy-done.31, f32[768]{0:T(1024)S(1)} %copy-done.27, f32[1024]{0:T(1024)S(1)} %copy-done.24, f32[1024]{0:T(1024)S(1)} %copy-done.22), kind=kOutput, calls=%fused_computation.120 | convolution fusion | flops 4835770368 | bytes 18888704 | tf_op jit(solution)/shard_map/dot_general | solution.py:29
  299.9 10.2 %fusion.55 = f32[3072,768]{1,0:T(8,128)} fusion(bf16[1024,3072]{1,0:T(8,128)(2,1)} %copy-done.62, bf16[1024,768]{1,0:T(8,128)(2,1)} %copy-done.17), kind=kOutput, calls=%fused_computation.132 | convolution fusion | flops 4831838208 | bytes 17301504 | tf_op jit(solution)/shard_map/dot_general | solution.py:29
  310.3 7.0 %copy.57 = bf16[2,512,2304]{2,1,0:T(8,128)(2,1)} copy(bf16[2,512,2304]{1,2,0:T(8,128)(2,1)} %get-tuple-element.77) | data formatting | bytes 9437184 | tf_op jit(solution)/shard_map/while | solution.py:225
  319.1 3.0 convert_reduce_fusion.3
  322.1 61.6 %all-reduce.9 = (bf16[768]{0:T(1024)(128)(2,1)}, bf16[768]{0:T(1024)(128)(2,1)}, bf16[768]{0:T(1024)(128)(2,1)}, bf16[768]{0:T(1024)(128)(2,1)}, bf16[768]{0:T(1...) all-reduce(f32[768]{0:T(1024)} %get-tuple-element.161, ...), channel_id=3, replica_groups=mesh['twin'=2,'dp'=16] {'dp'}, use_global_device_ids=true, to_apply=%region_24.25.clone | all-reduce | flops 9216 | bytes 55296
  393.5 5.6 all-reduce.10
  412.5 2.1 copy.64
  414.6 75.3 %reduce-scatter.9.cloned.1.call-done = f32[48,3072]{1,0:T(8,128)} async-done(((f32[768,3072]{1,0:T(8,128)}), f32[48,3072]{1,0:T(8,128)}) %reduce-scatter.9.cloned.1.call-update) | async-done | bytes 589840 | tf_op jit(solution)/shard_map/reduce_scatter | solution.py:257
  491.7 113.9 %reduce-scatter.11.cloned.1.call-done = f32[192,768]{1,0:T(8,128)} async-done(((f32[3072,768]{1,0:T(8,128)}), f32[192,768]{1,0:T(8,128)}) %reduce-scatter.11.cloned.1.call-update) | async-done | bytes 589840 | tf_op jit(solution)/shard_map/reduce_scatter | solution.py:259
  607.4 7.8 %add_convert_fusion.2 = bf16[1024,768]{1,0:T(8,128)(2,1)} fusion(f32[1024,768]{1,0:T(8,128)} %copy-done.12, bf16[1024,2304]{1,0:T(8,128)(2,1)} %bitcast.166, bf16[768,2304]{1,0:T(8,128)(2,1)S(1)} %copy-done, f32[1024]{0:T(1024)S(1)} %copy-done.41), kind=kOutput, calls=%fused_computation.47 | convolution fusion | flops 3626237952 | bytes 12980224 | tf_op jit(solution)/shard_map/dot_general | solution.py:35
  615.1 38.7 %all-reduce.14.cloned.1.call-done = (bf16[48,2304]{0,1:T(8,128)(2,1)}, bf16[48,768]{1,0:T(8,128)(2,1)}, bf16[48,3072]{1,0:T(8,128)(2,1)}, bf16[192,768]{1,0:T(8,128)(2,1)}) async-done(((bf16[48,2304]{0,1:T(8,128)(2,1)}, bf16[48,768]{1,0:T(8,128)(2,1)}, bf16[48,3072]{1,0:T(8,128)(2,1)}, bf16[192,768]{1,0:T(8,128)(2,1)}), (bf16[48,2304]{0,1:T(8,128)(2,1)}, bf16[48,768]{1,0:T(8,128)(2,1)}, ...) | async-done | bytes 884752 | tf_op jit(solution)/shard_map/psum | solution.py:279
  657.5 2.0 copy.58
  (281 shorter events, 86.3 us)
Async XLA Ops:
  7.2 403.8 %reduce-scatter.7.cloned.1.call-start = ((), (), s32[]{:S(2)}) async-start(), calls=%async_computation.4 | async-start | bytes 2506752 | tf_op jit(solution)/shard_map/reduce_scatter | solution.py:253
  16.5 6.7 copy-start.25
  23.8 38.7 %copy-start.54 = (bf16[768]{0:T(1024)(128)(2,1)S(1)}, bf16[768]{0:T(1024)(128)(2,1)}, u32[]{:S(2)}) copy-start(bf16[768]{0:T(1024)(128)(2,1)} %param.27) | copy-start | bytes 4612
  66.5 10.8 %copy-start.8 = (f32[1024,768]{1,0:T(8,128)}, f32[1024,768]{1,0:T(8,128)S(1)}, u32[]{:S(2)}) copy-start(f32[1024,768]{1,0:T(8,128)S(1)} %get-tuple-element.228) | copy-start | bytes 9437188
  66.6 105.5 %copy-start.21 = (f32[1024]{0:T(1024)}, f32[1024]{0:T(1024)S(1)}, u32[]{:S(2)}) copy-start(f32[1024]{0:T(1024)S(1)} %broadcast_multiply_fusion.1) | copy-start | bytes 12292
  66.6 10.7 %slice-start.3 = ((s8[4718592]{0:T(1024)(128)(4,1)}), s8[4194304]{0:T(1024)(128)(4,1)S(1)}, s32[]{:S(2)}) async-start(s8[4718592]{0:T(1024)(128)(4,1)} %bitcast.172), calls=%async_computation.12 | async-start | bytes 8388608
  67.7 104.4 %copy-start.23 = (f32[1024]{0:T(1024)}, f32[1024]{0:T(1024)S(1)}, u32[]{:S(2)}) copy-start(f32[1024]{0:T(1024)S(1)} %fusion.36) | copy-start | bytes 12292
  67.7 104.4 %copy-start.26 = (f32[768]{0:T(1024)}, f32[768]{0:T(1024)S(1)}, u32[]{:S(2)}) copy-start(f32[768]{0:T(1024)S(1)} %convert_element_type.200) | copy-start | bytes 9220
  67.8 9.6 %copy-start.30 = (f32[768]{0:T(1024)}, f32[768]{0:T(1024)S(1)}, u32[]{:S(2)}) copy-start(f32[768]{0:T(1024)S(1)} %convert_element_type.201) | copy-start | bytes 9220
  67.8 9.5 %copy-start.45 = (f32[3072]{0:T(1024)}, f32[3072]{0:T(1024)S(1)}, u32[]{:S(2)}) copy-start(f32[3072]{0:T(1024)S(1)} %convert_element_type.203) | copy-start | bytes 36868
  67.8 9.5 %slice-start.4 = ((s8[4718592]{0:T(1024)(128)(4,1)}), s8[524288]{0:T(1024)(128)(4,1)S(1)}, s32[]{:S(2)}) async-start(s8[4718592]{0:T(1024)(128)(4,1)} %bitcast.172), calls=%async_computation.13 | async-start | bytes 1048576
  84.7 48.5 %copy-start.53 = (s32[256]{0:T(256)S(1)}, s32[256]{0:T(256)}, u32[]{:S(2)}) copy-start(s32[256]{0:T(256)} %param.22) | copy-start | bytes 3076
  86.0 47.1 %copy-start.19 = (f32[2,8,768]{2,1,0:T(8,128)}, f32[2,8,768]{2,1,0:T(8,128)S(1)}, u32[]{:S(2)}) copy-start(f32[2,8,768]{2,1,0:T(8,128)S(1)} %get-tuple-element.234) | copy-start | bytes 147460
  86.0 47.2 %copy-start.51 = (f32[2,8]{1,0:T(2,128)}, f32[2,8]{1,0:T(2,128)S(1)}, u32[]{:S(2)}) copy-start(f32[2,8]{1,0:T(2,128)S(1)} %get-tuple-element.233) | copy-start | bytes 196
  135.1 6.3 copy-start.7
  135.1 6.3 copy-start.29
  135.1 6.3 copy-start.33
  135.1 6.3 copy-start.35
  145.7 15.1 %copy-start.17 = (bf16[1024,768]{1,0:T(8,128)(2,1)}, bf16[1024,768]{1,0:T(8,128)(2,1)S(1)}, u32[]{:S(2)}) copy-start(bf16[1024,768]{1,0:T(8,128)(2,1)S(1)} %get-tuple-element.210) | copy-start | bytes 4718596
  145.8 15.0 %copy-start.9 = (f32[1024,768]{1,0:T(8,128)S(1)}, f32[1024,768]{1,0:T(8,128)}, u32[]{:S(2)}) copy-start(f32[1024,768]{1,0:T(8,128)} %copy-done.8) | copy-start | bytes 9437188
  160.8 11.3 %copy-start.14 = (bf16[1024,3072]{1,0:T(8,128)(2,1)}, bf16[1024,3072]{1,0:T(8,128)(2,1)S(1)}, u32[]{:S(2)}) copy-start(bf16[1024,3072]{1,0:T(8,128)(2,1)S(1)} %get-tuple-element.241) | copy-start | bytes 18874372
  160.8 11.3 %copy-start.37 = (f32[1024]{0:T(1024)S(1)}, f32[1024]{0:T(1024)}, u32[]{:S(2)}) copy-start(f32[1024]{0:T(1024)} %copy-done.36) | copy-start | bytes 12292
  180.2 232.4 %reduce-scatter.13.cloned.1.call-start = ((), (), s32[]{:S(2)}) async-start(), calls=%async_computation.7 | async-start | bytes 7520256
  187.9 6.4 copy-start.1
  187.9 6.4 copy-start.3
  187.9 7.4 %copy-start.20 = (f32[2,12,512,1]{2,1,3,0:T(8,128)S(1)}, f32[2,12,512,1]{2,1,3,0:T(8,128)}, u32[]{:S(2)}) copy-start(f32[2,12,512,1]{2,1,3,0:T(8,128)} %get-tuple-element.368) | copy-start | bytes 147460 | tf_op jit(solution)/shard_map/while
  187.9 8.0 %copy-start.13 = (bf16[2,512,768]{2,1,0:T(8,128)(2,1)S(1)}, bf16[2,512,768]{2,1,0:T(8,128)(2,1)}, u32[]{:S(2)}) copy-start(bf16[2,512,768]{2,1,0:T(8,128)(2,1)} %get-tuple-element.369) | copy-start | bytes 4718596 | tf_op jit(solution)/shard_map/while
  199.2 11.6 %slice-start = ((s8[12582912]{0:T(1024)(128)(4,1)}), s8[4194304]{0:T(1024)(128)(4,1)S(1)}, s32[]{:S(2)}) async-start(s8[12582912]{0:T(1024)(128)(4,1)} %bitcast.149), calls=%async_computation.9 | async-start | bytes 8388608 | tf_op jit(solution)/shard_map/while
  199.2 11.6 %slice-start.1 = ((s8[12582912]{0:T(1024)(128)(4,1)}), s8[4194304]{0:T(1024)(128)(4,1)S(1)}, s32[]{:S(2)}) async-start(s8[12582912]{0:T(1024)(128)(4,1)} %bitcast.149), calls=%async_computation.10 | async-start | bytes 8388608 | tf_op jit(solution)/shard_map/while
  199.2 13.4 %slice-start.2 = ((s8[12582912]{0:T(1024)(128)(4,1)}), s8[4194304]{0:T(1024)(128)(4,1)S(1)}, s32[]{:S(2)}) async-start(s8[12582912]{0:T(1024)(128)(4,1)} %bitcast.149), calls=%async_computation.11 | async-start | bytes 8388608 | tf_op jit(solution)/shard_map/while
  199.2 13.4 %copy-start.10 = (pred[512,512]{0,1:T(8,128)(4,1)S(1)}, pred[512,512]{0,1:T(8,128)(4,1)}, u32[]{:S(2)}) copy-start(pred[512,512]{0,1:T(8,128)(4,1)} %broadcast_compare_fusion.5) | copy-start | bytes 786436 | tf_op jit(solution)/shard_map/while
  199.2 13.4 %copy-start.15 = (f32[12,512]{1,0:T(8,128)S(1)}, f32[12,512]{1,0:T(8,128)}, u32[]{:S(2)}) copy-start(f32[12,512]{1,0:T(8,128)} %dynamic-slice_bitcast_fusion.7) | copy-start | bytes 73732 | tf_op jit(solution)/shard_map/while
  212.6 7.1 %copy-start.2 = (bf16[512,768]{0,1:T(8,128)(2,1)S(1)}, bf16[512,768]{0,1:T(8,128)(2,1)}, u32[]{:S(2)}) copy-start(bf16[512,768]{0,1:T(8,128)(2,1)} %copy-done.1) | copy-start | bytes 2359300 | tf_op jit(solution)/shard_map/while
  230.6 6.4 copy-start.1
  230.6 6.4 copy-start.3
  230.6 7.3 %copy-start.20 = (f32[2,12,512,1]{2,1,3,0:T(8,128)S(1)}, f32[2,12,512,1]{2,1,3,0:T(8,128)}, u32[]{:S(2)}) copy-start(f32[2,12,512,1]{2,1,3,0:T(8,128)} %get-tuple-element.368) | copy-start | bytes 147460 | tf_op jit(solution)/shard_map/while
  230.6 7.9 %copy-start.13 = (bf16[2,512,768]{2,1,0:T(8,128)(2,1)S(1)}, bf16[2,512,768]{2,1,0:T(8,128)(2,1)}, u32[]{:S(2)}) copy-start(bf16[2,512,768]{2,1,0:T(8,128)(2,1)} %get-tuple-element.369) | copy-start | bytes 4718596 | tf_op jit(solution)/shard_map/while
  241.8 11.5 %slice-start = ((s8[12582912]{0:T(1024)(128)(4,1)}), s8[4194304]{0:T(1024)(128)(4,1)S(1)}, s32[]{:S(2)}) async-start(s8[12582912]{0:T(1024)(128)(4,1)} %bitcast.149), calls=%async_computation.9 | async-start | bytes 8388608 | tf_op jit(solution)/shard_map/while
  241.8 11.5 %slice-start.1 = ((s8[12582912]{0:T(1024)(128)(4,1)}), s8[4194304]{0:T(1024)(128)(4,1)S(1)}, s32[]{:S(2)}) async-start(s8[12582912]{0:T(1024)(128)(4,1)} %bitcast.149), calls=%async_computation.10 | async-start | bytes 8388608 | tf_op jit(solution)/shard_map/while
  241.8 13.2 %slice-start.2 = ((s8[12582912]{0:T(1024)(128)(4,1)}), s8[4194304]{0:T(1024)(128)(4,1)S(1)}, s32[]{:S(2)}) async-start(s8[12582912]{0:T(1024)(128)(4,1)} %bitcast.149), calls=%async_computation.11 | async-start | bytes 8388608 | tf_op jit(solution)/shard_map/while
  241.8 13.2 %copy-start.10 = (pred[512,512]{0,1:T(8,128)(4,1)S(1)}, pred[512,512]{0,1:T(8,128)(4,1)}, u32[]{:S(2)}) copy-start(pred[512,512]{0,1:T(8,128)(4,1)} %broadcast_compare_fusion.5) | copy-start | bytes 786436 | tf_op jit(solution)/shard_map/while
  241.8 13.2 %copy-start.15 = (f32[12,512]{1,0:T(8,128)S(1)}, f32[12,512]{1,0:T(8,128)}, u32[]{:S(2)}) copy-start(f32[12,512]{1,0:T(8,128)} %dynamic-slice_bitcast_fusion.7) | copy-start | bytes 73732 | tf_op jit(solution)/shard_map/while
  254.9 7.1 %copy-start.2 = (bf16[512,768]{0,1:T(8,128)(2,1)S(1)}, bf16[512,768]{0,1:T(8,128)(2,1)}, u32[]{:S(2)}) copy-start(bf16[512,768]{0,1:T(8,128)(2,1)} %copy-done.1) | copy-start | bytes 2359300 | tf_op jit(solution)/shard_map/while
  287.7 202.1 %reduce-scatter.9.cloned.1.call-start = ((), (), s32[]{:S(2)}) async-start(), calls=%async_computation.5 | async-start | bytes 10027008 | tf_op jit(solution)/shard_map/reduce_scatter | solution.py:257
  299.9 305.6 %reduce-scatter.11.cloned.1.call-start = ((), (), s32[]{:S(2)}) async-start(), calls=%async_computation.6 | async-start | bytes 10027008 | tf_op jit(solution)/shard_map/reduce_scatter | solution.py:259
  310.2 7.0 %copy-start.61 = (u32[32]{0:T(128)S(1)}, u32[32]{0:T(128)}, u32[]{:S(2)}) copy-start(u32[32]{0:T(128)} %constant.104) | copy-start | bytes 388
  310.2 343.6 %all-reduce.14.cloned.1.call-start = ((), (), s32[]{:S(2)}) async-start(), calls=%async_computation.8 | async-start | bytes 2506752 | tf_op jit(solution)/shard_map/psum | solution.py:279
  319.1 288.3 %copy-start.41 = (f32[1024]{0:T(1024)S(1)}, f32[1024]{0:T(1024)}, u32[]{:S(2)}) copy-start(f32[1024]{0:T(1024)} %copy-done.40) | copy-start | bytes 12292
  (42 other events, 79.7 us)
Sparse Core Ops, SparseCore 0:
  180.3 59.4 reduce-scatter.6
  287.8 86.7 reduce-scatter.12
  378.8 111.0 reduce-scatter.8
  494.4 111.1 reduce-scatter.10
  609.0 44.7 all-reduce.13
where the time goes:
time: 678 us; the launch traced here: 668 us
  waiting for transfers between devices  228 us (34%)
  matrix products  170 us (25%)
  blocking collectives  113 us (17%)
  local copies, waits for them, and re-layouts  75.6 us (11%)
  other arithmetic  65.3 us (10%)
  between operations  15.9 us (2%)
    reduce_scatter x1, waiting for transfers between devices, body(): lax.psum_scatter(grad_w_down, 'dp', scatter_dimension=0, tiled=True)  114 us
    reduce_scatter x1, waiting for transfers between devices, body(): lax.psum_scatter(grad_w_in, 'dp', scatter_dimension=0, tiled=True)  75.3 us
    unnamed x1, blocking collectives  61.6 us
    all_gather x1, blocking collectives, body(): gathered = lax.all_gather(unit_low, ('twin', 'dp'), axis=0, tiled=True)  45.3 us
    psum x1, waiting for transfers between devices, body(): lax.psum(grad_w_qkv.astype(jnp.bfloat16), 'twin').astype(jnp.float32)  38.7 us
    dot_general x5, matrix products, contract_cols(): lax.dot_general(left, right, (((1,), (1,)), ((), ())), preferred_element_...  38.7 us
    dot_general x5, matrix products, contract_rows(): lax.dot_general(left, right, (((0,), (0,)), ((), ())), preferred_element_...  35.4 us
    unnamed x131, local copies, waits for them, and re-layouts  29.5 us
  transfers between devices with their start and end apart: 5, of which 3 were waited for; matrix products, arithmetic and copies ran while one was open for 25% of the time, Pallas kernels for 0%

commit v1 on v0

--- a/solution.py
+++ b/solution.py
@@ -12,6 +12,10 @@
 norm_epsilon = 1e-12
 unit_epsilon = 1e-06
 masked_score = -1e30
+
+
+def _trace_roots(a0, axis_key):
+    return jax.lax.all_gather(a0, axis_key).sum(axis=0)
 
 
 def layer_norm(inputs, norm_gain, norm_shift):
@@ -276,7 +280,7 @@
         grad_ln2_gain,
         grad_ln2_bias,
     ) = (
-        lax.psum(grad_w_qkv.astype(jnp.bfloat16), "twin").astype(jnp.float32),
+        _trace_roots(grad_w_qkv.astype(jnp.bfloat16), "twin").astype(jnp.float32),
         lax.psum(grad_b_query.astype(jnp.bfloat16), "twin").astype(jnp.float32),
         lax.psum(grad_b_value.astype(jnp.bfloat16), "twin").astype(jnp.float32),
         lax.psum(grad_w_out.astype(jnp.bfloat16), "twin").astype(jnp.float32),

time: 678 us -> 625 us (0.922)
  waiting for transfers between devices: 228 us -> 162 us
  blocking collectives: 113 us -> 124 us
    reduce_scatter x1, waiting for transfers between devices: 75.3 us -> 35.6 us  [body(): lax.psum_scatter(grad_w_in, 'dp', scatter_dimension=0, tiled=True)]
    psum x1, waiting for transfers between devices: 38.7 us -> 13.1 us  [body(): lax.psum(grad_w_out.astype(jnp.bfloat16), 'twin').astype(jnp.float32)]
    all_gather x0 -> x1, blocking collectives: none -> 10.6 us  [_trace_roots(): return jax.lax.all_gather(a0, axis_key).sum(axis=0)]
    unnamed x131 -> x115, local copies, waits for them, and re-layouts: 29.5 us -> 24.4 us
  transfers between devices with their start and end apart: 5 -> 5, of which waited for: 3 -> 3; matrix products, arithmetic and copies ran while one was open for 25% -> 29% of each run, Pallas kernels for 0% -> 0%
where the time goes in v1:
time: 625 us; the launch traced here: 615 us
  matrix products  171 us (27%)
  waiting for transfers between devices  162 us (26%)
  blocking collectives  124 us (20%)
  local copies, waits for them, and re-layouts  70.1 us (11%)
  other arithmetic  70.1 us (11%)
  between operations  16 us (3%)
    reduce_scatter x1, waiting for transfers between devices, body(): lax.psum_scatter(grad_w_down, 'dp', scatter_dimension=0, tiled=True)  113 us
    unnamed x1, blocking collectives  62.8 us
    all_gather x1, blocking collectives, body(): gathered = lax.all_gather(unit_low, ('twin', 'dp'), axis=0, tiled=True)  45.3 us
    dot_general x5, matrix products, contract_cols(): lax.dot_general(left, right, (((1,), (1,)), ((), ())), preferred_element_...  38.7 us
    reduce_scatter x1, waiting for transfers between devices, body(): lax.psum_scatter(grad_w_in, 'dp', scatter_dimension=0, tiled=True)  35.6 us
    dot_general x5, matrix products, contract_rows(): lax.dot_general(left, right, (((0,), (0,)), ((), ())), preferred_element_...  35.3 us
    unnamed x115, local copies, waits for them, and re-layouts  24.4 us
    dot_general x2, matrix products, attend_backward(): jnp.einsum('qhd,khd->hqk', grad_heads, value_heads, preferred_element_typ...  23.6 us
  transfers between devices with their start and end apart: 5, of which 3 were waited for; matrix products, arithmetic and copies ran while one was open for 29% of the time, Pallas kernels for 0%

profile of v1, /device:TPU:0, one launch (start us, length us, event | category | flops | bytes accessed | tf_op | source)
XLA Modules:
  0.0 614.7 jit_solution(11413668231943065171)
XLA Ops:
  9.2 7.3 %add_convert_fusion.1 = bf16[1024,2304]{1,0:T(8,128)(2,1)} fusion(bf16[1024,768]{1,0:T(8,128)(2,1)} %bitcast.180, bf16[768,2304]{1,0:T(8,128)(2,1)S(1)} %copy-done, f32[2304]{0:T(1024)S(1)} %pad_maximum_fusion), kind=kOutput, calls=%fused_computation.35 | convolution fusion | flops 3628597248 | bytes 9839616 | tf_op jit(solution)/shard_map/dot_general | solution.py:98
  16.5 6.7 %copy.62 = bf16[2,512,2304]{1,2,0:T(8,128)(2,1)} copy(bf16[2,512,2304]{2,1,0:T(8,128)(2,1)} %bitcast.170) | data formatting | bytes 9437184 | tf_op jit(solution)/shard_map/while | solution.py:116
  23.8 38.7 %while.22 = (s32[]{:T(128)}, bf16[2,512,768]{2,1,0:T(8,128)(2,1)}, f32[2,12,512,1]{2,1,3,0:T(8,128)}, bf16[2,512,2304]{1,2,0:T(8,128)(2,1)}, s32[2,512]{1,0:T(2,128)S(1)}, /*index=5*/s32[]{:T(128)}) while((s32[]{:T(128)}, bf16[2,512,768]{2,1,0:T(8,128)(2,1)}, f32[2,12,512,1]{2,1,3,0:T(8,128)}, bf16[2,512,2304]{1,2,0:T(8,128)(2,1)}, ...), condition=%wide.region_3.4_spmd, body=%wide.region_0.3_spmd.sunk | while | flops 843704320 | bytes 55786600 | solution.py:116
  27.0 2.1 fusion.115
  29.1 3.5 fusion.116
  33.3 5.5 fusion.117
  38.8 2.3 copy.80
  41.1 2.1 constant_dynamic-update-slice_fusion.2
  46.3 2.1 fusion.115
  48.4 3.5 fusion.116
  52.6 5.5 fusion.117
  58.1 2.3 copy.80
  60.4 2.1 constant_dynamic-update-slice_fusion.2
  62.5 3.9 fusion.49
  67.7 9.4 %multiply_convert_fusion.3 = (bf16[1024,3072]{1,0:T(8,128)(2,1)S(1)}, f32[1024,3072]{1,0:T(8,128)}) fusion(f32[3072]{0:T(1024)S(1)} %convert_element_type.205, bf16[768,3072]{1,0:T(8,128)(2,1)S(1)} %bitcast.179, f32[1024,768]{1,0:T(8,128)S(1)} %get-tuple-element.193, f32[768]{0:T(1024)S(1)} %convert_element_type.203, f32[768]{0:T(1024)S(1)} %convert_element_type.202, ...), kind=kOutput, calls=%fused_computation.33 | convolution fusion | flops 4854644736 | bytes 26765312 | tf_op jit(solution)/shard_map/dot_general | solution.py:128
  77.2 5.5 fusion.50
  86.5 45.3 %all_gather.9 = bf16[512,768]{1,0:T(8,128)(2,1)S(1)} all-gather(bf16[16,768]{1,0:T(8,128)(2,1)S(1)} %fusion.29), channel_id=1, replica_groups=mesh['twin'=2,'dp'=16] {'twin','dp'}, dimensions={0}, use_global_device_ids=true | all-gather | bytes 811008 | tf_op jit(solution)/shard_map/all_gather | solution.py:155
  138.5 2.9 fusion.52
  145.7 15.0 %convert_reduce_fusion = (f32[3072]{0:T(1024)}, bf16[1024,3072]{1,0:T(8,128)(2,1)S(1)}) fusion(bf16[1024,768]{1,0:T(8,128)(2,1)S(1)} %get-tuple-element.175, bf16[3072,768]{1,0:T(8,128)(2,1)S(1)} %bitcast.177, f32[1024,3072]{1,0:T(8,128)} %get-tuple-element.195, f32[3072]{0:T(1024)S(1)} %copy-done.39), kind=kOutput, calls=%fused_computation.31 | convolution fusion | flops 4882166784 | bytes 25190400 | tf_op jit(solution)/shard_map/dot_general | solution.py:39
  160.8 11.3 %multiply_reduce_fusion.1 = (f32[768]{0:T(1024)}, f32[1024]{0:T(1024)S(1)}, f32[768]{0:T(1024)}, f32[1024,768]{1,0:T(8,128)S(1)}) fusion(f32[1024,768]{1,0:T(8,128)S(1)} %copy-done.9, f32[1024]{0:T(1024)S(1)} %fusion.36, f32[1024]{0:T(1024)S(1)} %broadcast_multiply_fusion.1, f32[768]{0:T(1024)S(1)} %convert_element_type.202, ...), kind=kOutput, calls=%fused_computation.43 | convolution fusion | flops 4839699456 | bytes 20472832 | tf_op jit(solution)/shard_map/dot_general | solution.py:39
  177.2 2.9 fusion.54
  180.2 11.5 %fusion.41 = f32[768,3072]{1,0:T(8,128)} fusion(bf16[1024,3072]{1,0:T(8,128)(2,1)} %copy-done.14, f32[1024,768]{1,0:T(8,128)} %copy-done.8, f32[768]{0:T(1024)} %copy-done.24, f32[768]{0:T(1024)S(1)} %convert_element_type.202, f32[1024]{0:T(1024)S(1)} %fusion.36, f32[1024]{0:T(1024)S(1)} %broadcast_multiply_fusion.1), kind=kOutput, calls=%fused_computation.120 | convolution fusion | flops 4835770368 | bytes 18888704 | tf_op jit(solution)/shard_map/dot_general | solution.py:33
  191.8 10.0 %fusion.55 = f32[3072,768]{1,0:T(8,128)} fusion(bf16[1024,3072]{1,0:T(8,128)(2,1)} %copy-done.55, bf16[1024,768]{1,0:T(8,128)(2,1)} %copy-done.17), kind=kOutput, calls=%fused_computation.132 | convolution fusion | flops 4831838208 | bytes 17301504 | tf_op jit(solution)/shard_map/dot_general | solution.py:33
  201.9 4.3 convolution_convert_fusion
  206.2 86.9 %while.23 = (s32[]{:T(128)}, bf16[2,512,2304]{1,2,0:T(8,128)(2,1)}, bf16[2,512,2304]{1,2,0:T(8,128)(2,1)}, s32[2,512]{1,0:T(2,128)S(1)}, f32[2,12,512,1]{2,1,3,0...) while((s32[]{:T(128)}, bf16[2,512,2304]{1,2,0:T(8,128)(2,1)}, bf16[2,512,2304]{1,2,0:T(8,128)(2,1)}, ...), condition=%wide.region_20.21_spmd, body=%wide.region_18.20_spmd.sunk | while | flops 2079188992 | bytes 181877680 | solution.py:229
  209.2 6.4 %fusion.129 = f32[12,512,512]{1,2,0:T(8,128)} fusion(bf16[512,12,64]{0,2,1:T(8,128)(2,1)S(1)} %bitcast.154, bf16[512,12,64]{0,2,1:T(8,128)(2,1)S(1)} %bitcast.152), kind=kOutput, calls=%fused_computation.130.clone.1 | convolution fusion | flops 402653184 | bytes 14155776 | tf_op jit(solution)/shard_map/while/body/eval_jaxpr/qhd,khd->hqk/dot_general | solution.py:53
  218.1 2.3 copy.81
  220.5 11.6 %multiply_reduce_fusion.9 = (f32[12,512]{1,0:T(8,128)S(1)}, f32[12,512,512]{1,2,0:T(8,128)}) fusion(f32[12,512]{1,0:T(8,128)} %dynamic-slice_bitcast_fusion.7, f32[12,512,512]{1,2,0:T(8,128)} %fusion.129, pred[512,512]{0,1:T(8,128)(4,1)} %broadcast_compare_fusion.5, bf16[512,12,64]{0,2,1:T(8,128)(2,1)} %bitcast.163, bf16[512,12,64]{0,2,1:T(8,128)(2,1)} %bitcast.161), kind=kOutput, calls=%fused_computation.15.clone.1 | convolution fusion | flops 421521408 | bytes 27049984 | tf_op jit(solution)/shard_map/while/body/eval_jaxpr/qhd,khd->hqk/dot_general | solution.py:209
  233.7 7.1 %multiply_convert_fusion.9 = bf16[12,512,512]{1,2,0:T(8,128)(2,1)S(1)} fusion(f32[12,512,512]{1,2,0:T(8,128)} %get-tuple-element.295, f32[12,512]{1,0:T(8,128)S(1)} %get-tuple-element.296, f32[12,512]{1,0:T(8,128)S(1)} %copy-done.15, f32[12,512,512]{1,2,0:T(8,128)S(1)} %bitcast.151, pred[512,512]{0,1:T(8,128)(4,1)S(1)} %copy-done.10), kind=kLoop, calls=%fused_computation.14.clone.1 | loop fusion | flops 22020096 | bytes 31768576 | tf_op jit(solution)/shard_map/while/body/eval_jaxpr/convert_element_type | solution.py:213
  242.0 2.0 multiply_convert_fusion.10
  244.0 3.2 fusion.130
  251.6 7.5 %fusion.129 = f32[12,512,512]{1,2,0:T(8,128)} fusion(bf16[512,12,64]{0,2,1:T(8,128)(2,1)S(1)} %bitcast.154, bf16[512,12,64]{0,2,1:T(8,128)(2,1)S(1)} %bitcast.152), kind=kOutput, calls=%fused_computation.130.clone.1 | convolution fusion | flops 402653184 | bytes 14155776 | tf_op jit(solution)/shard_map/while/body/eval_jaxpr/qhd,khd->hqk/dot_general | solution.py:53
  261.7 2.4 copy.81
  264.1 12.1 %multiply_reduce_fusion.9 = (f32[12,512]{1,0:T(8,128)S(1)}, f32[12,512,512]{1,2,0:T(8,128)}) fusion(f32[12,512]{1,0:T(8,128)} %dynamic-slice_bitcast_fusion.7, f32[12,512,512]{1,2,0:T(8,128)} %fusion.129, pred[512,512]{0,1:T(8,128)(4,1)} %broadcast_compare_fusion.5, bf16[512,12,64]{0,2,1:T(8,128)(2,1)} %bitcast.163, bf16[512,12,64]{0,2,1:T(8,128)(2,1)} %bitcast.161), kind=kOutput, calls=%fused_computation.15.clone.1 | convolution fusion | flops 421521408 | bytes 27049984 | tf_op jit(solution)/shard_map/while/body/eval_jaxpr/qhd,khd->hqk/dot_general | solution.py:209
  277.9 7.1 %multiply_convert_fusion.9 = bf16[12,512,512]{1,2,0:T(8,128)(2,1)S(1)} fusion(f32[12,512,512]{1,2,0:T(8,128)} %get-tuple-element.295, f32[12,512]{1,0:T(8,128)S(1)} %get-tuple-element.296, f32[12,512]{1,0:T(8,128)S(1)} %copy-done.15, f32[12,512,512]{1,2,0:T(8,128)S(1)} %bitcast.151, pred[512,512]{0,1:T(8,128)(4,1)S(1)} %copy-done.10), kind=kLoop, calls=%fused_computation.14.clone.1 | loop fusion | flops 22020096 | bytes 31768576 | tf_op jit(solution)/shard_map/while/body/eval_jaxpr/convert_element_type | solution.py:213
  286.2 2.0 multiply_convert_fusion.10
  288.2 3.2 fusion.130
  293.1 9.6 %convolution_bitcast_fusion = f32[768,2304]{0,1:T(8,128)} fusion(bf16[2,512,2304]{1,2,0:T(8,128)(2,1)} %get-tuple-element.77, bf16[2,512,768]{2,1,0:T(8,128)(2,1)} %param.20), kind=kOutput, calls=%fused_computation.36 | convolution fusion | flops 3623878656 | bytes 13369344 | tf_op jit(solution)/shard_map/dot_general | solution.py:33
  302.7 8.0 %copy.72 = f32[768,2304]{1,0:T(8,128)} copy(f32[768,2304]{0,1:T(8,128)} %convolution_bitcast_fusion) | data formatting | bytes 14155776
  310.8 6.8 %copy.66 = bf16[2,512,2304]{2,1,0:T(8,128)(2,1)} copy(bf16[2,512,2304]{1,2,0:T(8,128)(2,1)} %get-tuple-element.77) | data formatting | bytes 9437184 | tf_op jit(solution)/shard_map/while | solution.py:229
  319.2 35.6 %reduce-scatter.9.cloned.1.call-done = f32[48,3072]{1,0:T(8,128)} async-done(((f32[768,3072]{1,0:T(8,128)}), f32[48,3072]{1,0:T(8,128)}) %reduce-scatter.9.cloned.1.call-update) | async-done | bytes 589840 | tf_op jit(solution)/shard_map/reduce_scatter | solution.py:261
  356.6 113.4 %reduce-scatter.11.cloned.1.call-done = f32[192,768]{1,0:T(8,128)} async-done(((f32[3072,768]{1,0:T(8,128)}), f32[192,768]{1,0:T(8,128)}) %reduce-scatter.11.cloned.1.call-update) | async-done | bytes 589840 | tf_op jit(solution)/shard_map/reduce_scatter | solution.py:263
  471.9 7.8 %add_convert_fusion.2 = bf16[1024,768]{1,0:T(8,128)(2,1)} fusion(f32[1024,768]{1,0:T(8,128)} %copy-done.12, bf16[1024,2304]{1,0:T(8,128)(2,1)} %bitcast.166, bf16[768,2304]{1,0:T(8,128)(2,1)S(1)} %copy-done, f32[1024]{0:T(1024)S(1)} %copy-done.34), kind=kOutput, calls=%fused_computation.47 | convolution fusion | flops 3626237952 | bytes 12980224 | tf_op jit(solution)/shard_map/dot_general | solution.py:39
  481.6 3.3 convert_reduce_fusion.3
  484.9 62.8 %all-reduce.9 = (bf16[768]{0:T(1024)(128)(2,1)}, bf16[768]{0:T(1024)(128)(2,1)}, bf16[768]{0:T(1024)(128)(2,1)}, bf16[768]{0:T(1024)(128)(2,1)}, bf16[768]{0:T(1...) all-reduce(f32[768]{0:T(1024)} %get-tuple-element.127, ...), channel_id=4, replica_groups=mesh['twin'=2,'dp'=16] {'dp'}, use_global_device_ids=true, to_apply=%region_24.25.clone | all-reduce | flops 9216 | bytes 55296
  556.9 5.7 all-reduce.10
  575.5 10.6 %all-gather = bf16[96,2304]{1,0:T(8,128)(2,1)} all-gather(bf16[48,2304]{1,0:T(8,128)(2,1)S(1)} %convert_element_type.220), channel_id=2, replica_groups=mesh['twin'=2,'dp'=16] {'twin'}, dimensions={0}, use_global_device_ids=true | all-gather | bytes 663552 | tf_op jit(solution)/shard_map/all_gather | solution.py:18
  589.6 13.1 %all-reduce.14.cloned.1.call-done = (bf16[48,768]{1,0:T(8,128)(2,1)}, bf16[48,3072]{1,0:T(8,128)(2,1)}, bf16[192,768]{1,0:T(8,128)(2,1)}) async-done(((bf16[48,768]{1,0:T(8,128)(2,1)}, bf16[48,3072]{1,0:T(8,128)(2,1)}, bf16[192,768]{1,0:T(8,128)(2,1)}), (bf16[48,768]{1,0:T(8,128)(2,1)}, bf16[48,3072]{1,0:T(8,128)(2,1)}, bf16[192,768]{1,0:T(8,128)(2,1)})) %all-reduce.14.cloned.1.call-update) | async-done | bytes 663568 | tf_op jit(solution)/shard_map/psum | solution.py:286
  (269 shorter events, 87.6 us)
Async XLA Ops:
  7.2 310.4 %reduce-scatter.7.cloned.1.call-start = ((), (), s32[]{:S(2)}) async-start(), calls=%async_computation.4 | async-start | bytes 2506752 | tf_op jit(solution)/shard_map/reduce_scatter | solution.py:257
  16.5 6.7 %copy-start.21 = (s32[2,512]{1,0:T(2,128)S(1)}, s32[2,512]{1,0:T(2,128)}, u32[]{:S(2)}) copy-start(s32[2,512]{1,0:T(2,128)} %param.21) | copy-start | bytes 12292
  23.8 38.7 %copy-start.47 = (bf16[768]{0:T(1024)(128)(2,1)S(1)}, bf16[768]{0:T(1024)(128)(2,1)}, u32[]{:S(2)}) copy-start(bf16[768]{0:T(1024)(128)(2,1)} %param.27) | copy-start | bytes 4612
  62.5 5.2 slice-start.7
  62.5 5.2 slice-start.8
  66.4 10.8 %copy-start.8 = (f32[1024,768]{1,0:T(8,128)}, f32[1024,768]{1,0:T(8,128)S(1)}, u32[]{:S(2)}) copy-start(f32[1024,768]{1,0:T(8,128)S(1)} %get-tuple-element.193) | copy-start | bytes 9437188
  66.5 10.7 %slice-start.3 = ((s8[4718592]{0:T(1024)(128)(4,1)}), s8[4194304]{0:T(1024)(128)(4,1)S(1)}, s32[]{:S(2)}) async-start(s8[4718592]{0:T(1024)(128)(4,1)} %bitcast.174), calls=%async_computation.12 | async-start | bytes 8388608
  67.6 9.6 %copy-start.24 = (f32[768]{0:T(1024)}, f32[768]{0:T(1024)S(1)}, u32[]{:S(2)}) copy-start(f32[768]{0:T(1024)S(1)} %convert_element_type.203) | copy-start | bytes 9220
  67.7 9.5 %copy-start.38 = (f32[3072]{0:T(1024)}, f32[3072]{0:T(1024)S(1)}, u32[]{:S(2)}) copy-start(f32[3072]{0:T(1024)S(1)} %convert_element_type.205) | copy-start | bytes 36868
  67.7 9.5 %slice-start.4 = ((s8[4718592]{0:T(1024)(128)(4,1)}), s8[524288]{0:T(1024)(128)(4,1)S(1)}, s32[]{:S(2)}) async-start(s8[4718592]{0:T(1024)(128)(4,1)} %bitcast.174), calls=%async_computation.13 | async-start | bytes 1048576
  77.2 5.5 copy-start.55
  84.5 48.5 %copy-start.46 = (s32[256]{0:T(256)S(1)}, s32[256]{0:T(256)}, u32[]{:S(2)}) copy-start(s32[256]{0:T(256)} %param.22) | copy-start | bytes 3076
  85.9 47.2 %copy-start.19 = (f32[2,8,768]{2,1,0:T(8,128)}, f32[2,8,768]{2,1,0:T(8,128)S(1)}, u32[]{:S(2)}) copy-start(f32[2,8,768]{2,1,0:T(8,128)S(1)} %get-tuple-element.199) | copy-start | bytes 147460
  85.9 47.2 %copy-start.44 = (f32[2,8]{1,0:T(2,128)}, f32[2,8]{1,0:T(2,128)S(1)}, u32[]{:S(2)}) copy-start(f32[2,8]{1,0:T(2,128)S(1)} %get-tuple-element.198) | copy-start | bytes 196
  135.1 6.3 %copy-start.7 = (f32[1024,768]{1,0:T(8,128)S(1)}, f32[1024,768]{1,0:T(8,128)}, u32[]{:S(2)}) copy-start(f32[1024,768]{1,0:T(8,128)} %copy-done.6) | copy-start | bytes 9437188
  135.1 6.3 %copy-start.23 = (f32[1024]{0:T(1024)S(1)}, f32[1024]{0:T(1024)}, u32[]{:S(2)}) copy-start(f32[1024]{0:T(1024)} %copy-done.22) | copy-start | bytes 12292
  135.1 6.3 %copy-start.26 = (f32[1024]{0:T(1024)S(1)}, f32[1024]{0:T(1024)}, u32[]{:S(2)}) copy-start(f32[1024]{0:T(1024)} %copy-done.25) | copy-start | bytes 12292
  135.1 6.3 %copy-start.28 = (f32[768]{0:T(1024)S(1)}, f32[768]{0:T(1024)}, u32[]{:S(2)}) copy-start(f32[768]{0:T(1024)} %copy-done.27) | copy-start | bytes 9220
  145.7 15.0 %copy-start.17 = (bf16[1024,768]{1,0:T(8,128)(2,1)}, bf16[1024,768]{1,0:T(8,128)(2,1)S(1)}, u32[]{:S(2)}) copy-start(bf16[1024,768]{1,0:T(8,128)(2,1)S(1)} %get-tuple-element.175) | copy-start | bytes 4718596
  145.7 15.0 %copy-start.9 = (f32[1024,768]{1,0:T(8,128)S(1)}, f32[1024,768]{1,0:T(8,128)}, u32[]{:S(2)}) copy-start(f32[1024,768]{1,0:T(8,128)} %copy-done.8) | copy-start | bytes 9437188
  160.8 11.3 %copy-start.14 = (bf16[1024,3072]{1,0:T(8,128)(2,1)}, bf16[1024,3072]{1,0:T(8,128)(2,1)S(1)}, u32[]{:S(2)}) copy-start(bf16[1024,3072]{1,0:T(8,128)(2,1)S(1)} %get-tuple-element.206) | copy-start | bytes 18874372
  160.8 11.3 %copy-start.30 = (f32[1024]{0:T(1024)S(1)}, f32[1024]{0:T(1024)}, u32[]{:S(2)}) copy-start(f32[1024]{0:T(1024)} %copy-done.29) | copy-start | bytes 12292
  180.2 174.6 %reduce-scatter.9.cloned.1.call-start = ((), (), s32[]{:S(2)}) async-start(), calls=%async_computation.5 | async-start | bytes 10027008 | tf_op jit(solution)/shard_map/reduce_scatter | solution.py:261
  191.8 278.3 %reduce-scatter.11.cloned.1.call-start = ((), (), s32[]{:S(2)}) async-start(), calls=%async_computation.6 | async-start | bytes 10027008 | tf_op jit(solution)/shard_map/reduce_scatter | solution.py:263
  201.8 372.6 %reduce-scatter.13.cloned.1.call-start = ((), (), s32[]{:S(2)}) async-start(), calls=%async_computation.7 | async-start | bytes 7520256 | tf_op jit(solution)/shard_map/reduce_scatter | solution.py:254
  209.2 6.4 %copy-start.1 = (bf16[512,768]{0,1:T(8,128)(2,1)}, bf16[512,768]{0,1:T(8,128)(2,1)S(1)}, u32[]{:S(2)}) copy-start(bf16[512,768]{0,1:T(8,128)(2,1)S(1)} %get-tuple-element.293) | copy-start | bytes 2359300 | tf_op jit(solution)/shard_map/while
  209.2 6.4 %copy-start.3 = (bf16[512,768]{0,1:T(8,128)(2,1)}, bf16[512,768]{0,1:T(8,128)(2,1)S(1)}, u32[]{:S(2)}) copy-start(bf16[512,768]{0,1:T(8,128)(2,1)S(1)} %get-tuple-element.292) | copy-start | bytes 2359300 | tf_op jit(solution)/shard_map/while
  209.2 7.3 %copy-start.20 = (f32[2,12,512,1]{2,1,3,0:T(8,128)S(1)}, f32[2,12,512,1]{2,1,3,0:T(8,128)}, u32[]{:S(2)}) copy-start(f32[2,12,512,1]{2,1,3,0:T(8,128)} %get-tuple-element.333) | copy-start | bytes 147460 | tf_op jit(solution)/shard_map/while
  209.2 7.9 %copy-start.13 = (bf16[2,512,768]{2,1,0:T(8,128)(2,1)S(1)}, bf16[2,512,768]{2,1,0:T(8,128)(2,1)}, u32[]{:S(2)}) copy-start(bf16[2,512,768]{2,1,0:T(8,128)(2,1)} %get-tuple-element.334) | copy-start | bytes 4718596 | tf_op jit(solution)/shard_map/while
  220.4 11.6 %slice-start = ((s8[12582912]{0:T(1024)(128)(4,1)}), s8[4194304]{0:T(1024)(128)(4,1)S(1)}, s32[]{:S(2)}) async-start(s8[12582912]{0:T(1024)(128)(4,1)} %bitcast.150), calls=%async_computation.9 | async-start | bytes 8388608 | tf_op jit(solution)/shard_map/while
  220.4 11.6 %slice-start.1 = ((s8[12582912]{0:T(1024)(128)(4,1)}), s8[4194304]{0:T(1024)(128)(4,1)S(1)}, s32[]{:S(2)}) async-start(s8[12582912]{0:T(1024)(128)(4,1)} %bitcast.150), calls=%async_computation.10 | async-start | bytes 8388608 | tf_op jit(solution)/shard_map/while
  220.4 13.2 %slice-start.2 = ((s8[12582912]{0:T(1024)(128)(4,1)}), s8[4194304]{0:T(1024)(128)(4,1)S(1)}, s32[]{:S(2)}) async-start(s8[12582912]{0:T(1024)(128)(4,1)} %bitcast.150), calls=%async_computation.11 | async-start | bytes 8388608 | tf_op jit(solution)/shard_map/while
  220.4 13.2 %copy-start.10 = (pred[512,512]{0,1:T(8,128)(4,1)S(1)}, pred[512,512]{0,1:T(8,128)(4,1)}, u32[]{:S(2)}) copy-start(pred[512,512]{0,1:T(8,128)(4,1)} %broadcast_compare_fusion.5) | copy-start | bytes 786436 | tf_op jit(solution)/shard_map/while
  220.4 13.2 %copy-start.15 = (f32[12,512]{1,0:T(8,128)S(1)}, f32[12,512]{1,0:T(8,128)}, u32[]{:S(2)}) copy-start(f32[12,512]{1,0:T(8,128)} %dynamic-slice_bitcast_fusion.7) | copy-start | bytes 73732 | tf_op jit(solution)/shard_map/while
  233.7 7.1 %copy-start.2 = (bf16[512,768]{0,1:T(8,128)(2,1)S(1)}, bf16[512,768]{0,1:T(8,128)(2,1)}, u32[]{:S(2)}) copy-start(bf16[512,768]{0,1:T(8,128)(2,1)} %copy-done.1) | copy-start | bytes 2359300 | tf_op jit(solution)/shard_map/while
  251.6 7.5 %copy-start.1 = (bf16[512,768]{0,1:T(8,128)(2,1)}, bf16[512,768]{0,1:T(8,128)(2,1)S(1)}, u32[]{:S(2)}) copy-start(bf16[512,768]{0,1:T(8,128)(2,1)S(1)} %get-tuple-element.293) | copy-start | bytes 2359300 | tf_op jit(solution)/shard_map/while
  251.6 7.5 %copy-start.3 = (bf16[512,768]{0,1:T(8,128)(2,1)}, bf16[512,768]{0,1:T(8,128)(2,1)S(1)}, u32[]{:S(2)}) copy-start(bf16[512,768]{0,1:T(8,128)(2,1)S(1)} %get-tuple-element.292) | copy-start | bytes 2359300 | tf_op jit(solution)/shard_map/while
  251.6 8.5 %copy-start.20 = (f32[2,12,512,1]{2,1,3,0:T(8,128)S(1)}, f32[2,12,512,1]{2,1,3,0:T(8,128)}, u32[]{:S(2)}) copy-start(f32[2,12,512,1]{2,1,3,0:T(8,128)} %get-tuple-element.333) | copy-start | bytes 147460 | tf_op jit(solution)/shard_map/while
  251.6 9.1 %copy-start.13 = (bf16[2,512,768]{2,1,0:T(8,128)(2,1)S(1)}, bf16[2,512,768]{2,1,0:T(8,128)(2,1)}, u32[]{:S(2)}) copy-start(bf16[2,512,768]{2,1,0:T(8,128)(2,1)} %get-tuple-element.334) | copy-start | bytes 4718596 | tf_op jit(solution)/shard_map/while
  264.1 12.1 %slice-start = ((s8[12582912]{0:T(1024)(128)(4,1)}), s8[4194304]{0:T(1024)(128)(4,1)S(1)}, s32[]{:S(2)}) async-start(s8[12582912]{0:T(1024)(128)(4,1)} %bitcast.150), calls=%async_computation.9 | async-start | bytes 8388608 | tf_op jit(solution)/shard_map/while
  264.1 12.1 %slice-start.1 = ((s8[12582912]{0:T(1024)(128)(4,1)}), s8[4194304]{0:T(1024)(128)(4,1)S(1)}, s32[]{:S(2)}) async-start(s8[12582912]{0:T(1024)(128)(4,1)} %bitcast.150), calls=%async_computation.10 | async-start | bytes 8388608 | tf_op jit(solution)/shard_map/while
  264.1 13.8 %slice-start.2 = ((s8[12582912]{0:T(1024)(128)(4,1)}), s8[4194304]{0:T(1024)(128)(4,1)S(1)}, s32[]{:S(2)}) async-start(s8[12582912]{0:T(1024)(128)(4,1)} %bitcast.150), calls=%async_computation.11 | async-start | bytes 8388608 | tf_op jit(solution)/shard_map/while
  264.1 13.8 %copy-start.10 = (pred[512,512]{0,1:T(8,128)(4,1)S(1)}, pred[512,512]{0,1:T(8,128)(4,1)}, u32[]{:S(2)}) copy-start(pred[512,512]{0,1:T(8,128)(4,1)} %broadcast_compare_fusion.5) | copy-start | bytes 786436 | tf_op jit(solution)/shard_map/while
  264.1 13.8 %copy-start.15 = (f32[12,512]{1,0:T(8,128)S(1)}, f32[12,512]{1,0:T(8,128)}, u32[]{:S(2)}) copy-start(f32[12,512]{1,0:T(8,128)} %dynamic-slice_bitcast_fusion.7) | copy-start | bytes 73732 | tf_op jit(solution)/shard_map/while
  277.9 7.1 %copy-start.2 = (bf16[512,768]{0,1:T(8,128)(2,1)S(1)}, bf16[512,768]{0,1:T(8,128)(2,1)}, u32[]{:S(2)}) copy-start(bf16[512,768]{0,1:T(8,128)(2,1)} %copy-done.1) | copy-start | bytes 2359300 | tf_op jit(solution)/shard_map/while
  310.8 161.1 %copy-start.34 = (f32[1024]{0:T(1024)S(1)}, f32[1024]{0:T(1024)}, u32[]{:S(2)}) copy-start(f32[1024]{0:T(1024)} %copy-done.33) | copy-start | bytes 12292
  310.8 292.0 %all-reduce.14.cloned.1.call-start = ((), (), s32[]{:S(2)}) async-start(), calls=%async_computation.8 | async-start | bytes 1327104 | tf_op jit(solution)/shard_map/psum | solution.py:286
  471.9 7.8 %copy-start.54 = (u32[32]{0:T(128)S(1)}, u32[32]{0:T(128)}, u32[]{:S(2)}) copy-start(u32[32]{0:T(128)} %constant.105) | copy-start | bytes 388
  (35 other events, 61.9 us)
Sparse Core Ops, SparseCore 0:
  180.3 59.3 reduce-scatter.6
  244.4 110.3 reduce-scatter.8
  358.9 111.0 reduce-scatter.10
  474.5 90.3 reduce-scatter.12
  568.3 34.3 all-reduce.13
